TPU v7x, 128 devices: a whole 4x4x4 slice. The times are simulated.
128 devices in a mesh: section: 2 (over x_hi), seq: 16 (over z, y), mp: 4 (over x_lo, core).
Axes of the slice: x: 4 (x_hi: 2, x_lo: 2; x = x_hi * 2 + x_lo), y: 4, z: 4, core: 2. Of those that a mesh axis runs over, the one named last changes fastest.
Arguments:
- video: bfloat16 [2, 4, 128, 3072], P(None, None, 'seq'), may hold values from -6 to 6
- text: bfloat16 [2, 128, 3072], P(None, 'seq'), may hold values from -6 to 6
- patch_lengths: int32 [2, 4], replicated, may hold values from 1 to 128, 384 in all within a row
- text_len: int32 [2], replicated, may hold values from 64 to 128, as said below
- timestep: int32 [1], replicated, may hold values from 0 to 999
- w_mod: bfloat16 [2, 512, 9216], P('section', None, 'mp'), may hold values from -0.25 to 0.25
- w_qkv: bfloat16 [2, 3072, 3, 3072], P('section', None, None, 'mp')
- w_out: bfloat16 [2, 3072, 3072], P('section', 'mp'), may hold values from -0.109375 to 0.109375
- stale_cache: bfloat16 [2, 2, 4, 128, 2, 3072], P('section', None, None, 'seq', None, 'mp'), may hold values from -6 to 6
Outputs:
- hidden_video: bfloat16 [2, 2, 4, 128, 3072], P('section', None, None, 'seq')
- hidden_text: bfloat16 [2, 2, 128, 3072], P('section', None, 'seq')
- cache_video: bfloat16 [2, 2, 4, 128, 2, 3072], P('section', None, None, 'seq', None, 'mp')
- cache_text: bfloat16 [2, 2, 128, 2, 3072], P('section', None, 'seq', None, 'mp')
Inputs may be any that keep to these rules, and one draw needn't show every extreme that they name: `patch_lengths`: 4 patch lengths per request summing to 384; in every request the largest is 128. `text_len`: exactly one request has 128, every other fewer.
All inputs are finite; a program needn't handle non-finite values.
Results may differ from a plain program's by a relative error of at most 0.01.
Values may be sent and summed in bfloat16 or wider, within the bound.
No kernel may reach another device: no remote copies, remote signals or barrier semaphores. Data moves between devices by JAX's collectives and lax.ppermute only.
A program may use at most 192 MiB of HBM per device.

v0:
```python
import math
import jax
import jax.numpy as jnp
from jax import lax
from jax.sharding import PartitionSpec as P

HEAD = 64
EPS = 1e-05
NEG = -1e30


def passed_along(value, axis, steps):
    count = lax.axis_size(axis)
    leading, last = (max(0, -steps), min(count, count - steps))
    return lax.ppermute(value, axis, [(source, source + steps) for source in range(leading, last)])


def modulation(timestep, weight):
    half_width = weight.shape[0] // 2
    frequency = jnp.exp(-math.log(10000.0) * jnp.arange(half_width, dtype=jnp.float32) / half_width)
    phases = timestep.astype(jnp.float32)[0] * frequency
    embedding = jnp.concatenate([jnp.cos(phases), jnp.sin(phases)])
    active = jax.nn.silu(embedding).astype(jnp.bfloat16)
    return jnp.dot(active[None, :], weight, preferred_element_type=jnp.float32)[0]


def normalize(token_rows, shift_vec, scale_vec):
    values = token_rows.astype(jnp.float32)
    center = values - jnp.mean(values, axis=-1, keepdims=True)
    spread = jnp.mean(center * center, axis=-1, keepdims=True)
    return (center * lax.rsqrt(spread + EPS) * (1.0 + scale_vec) + shift_vec).astype(jnp.bfloat16)


def scores_of(query_heads, key_value, head_count):
    requests, key_count = (key_value.shape[0], key_value.shape[1])
    key_heads = key_value[:, :, 0].reshape(requests, key_count, head_count, HEAD)
    value_heads = key_value[:, :, 1].reshape(requests, key_count, head_count, HEAD)
    scores = jnp.einsum(
        "rqhe,rkhe->rhqk", query_heads, key_heads, preferred_element_type=jnp.float32
    ) * HEAD ** (-0.5)
    return (scores, value_heads)


def masked_max(scores, key_mask):
    return jnp.max(jnp.where(key_mask[:, None, None, :], scores, NEG), axis=-1)


def weighed(scores, key_mask, top_score, value_heads):
    weights = jnp.where(key_mask[:, None, None, :], jnp.exp(scores - top_score[..., None]), 0.0)
    weight_sum = jnp.sum(weights, axis=-1)
    accumulated = jnp.einsum(
        "rhqk,rkhe->rhqe",
        weights.astype(jnp.bfloat16),
        value_heads,
        preferred_element_type=jnp.float32,
    )
    return (weight_sum, accumulated)


def body(video, text, patch_lengths, text_len, timestep, w_mod, w_qkv, w_out, stale_cache):
    section_index = lax.axis_index("section")
    seq_count = lax.axis_size("seq")
    requests, patches, per_dev, model_width = video.shape
    text_dev = text.shape[1]
    capacity = per_dev * seq_count
    text_slots = text_dev * seq_count
    column_count = w_out.shape[1]
    head_count = column_count // HEAD
    row_count = per_dev + text_dev
    modulated = lax.all_gather(modulation(timestep, w_mod[0]), "mp", axis=0, tiled=True)
    shift_vec = modulated[:model_width]
    scale_vec = modulated[model_width : 2 * model_width]
    gate_vec = modulated[2 * model_width :]
    weight_qkv = w_qkv[0].reshape(model_width, 3 * column_count)
    weight_out = w_out[0]
    stale_local = stale_cache[0]
    slot_index = jnp.arange(capacity, dtype=jnp.int32)
    video_valid = (slot_index[None, None, :] < patch_lengths[:, :, None]).reshape(requests, -1)
    text_valid = jnp.arange(text_slots, dtype=jnp.int32)[None, :] < text_len[:, None]
    all_valid = jnp.concatenate([video_valid, text_valid], axis=1)
    video_patch = jnp.repeat(jnp.arange(patches, dtype=jnp.int32), capacity)
    all_patch = jnp.concatenate([video_patch, jnp.zeros((text_slots,), jnp.int32)])
    stale_whole = lax.all_gather(stale_local, "seq", axis=2, tiled=True).reshape(
        requests, patches * capacity, 2, column_count
    )
    fresh_video = jnp.zeros((requests, patches, capacity, 2, column_count), jnp.bfloat16)
    fresh_text = jnp.zeros((requests, text_slots, 2, column_count), jnp.bfloat16)
    own_video = jnp.zeros((requests, patches, per_dev, 2, column_count), jnp.bfloat16)
    own_text = jnp.zeros((requests, text_dev, 2, column_count), jnp.bfloat16)
    out_video = jnp.zeros((requests, patches, per_dev, model_width), jnp.bfloat16)
    out_text = jnp.zeros((requests, text_dev, model_width), jnp.bfloat16)
    received = jnp.zeros((requests, row_count, model_width), jnp.bfloat16)
    patch_ids = jnp.arange(patches, dtype=jnp.int32)
    for turn_index in range(patches + 1):
        patch_now = turn_index - section_index
        picked = lax.dynamic_index_in_dim(
            video, jnp.clip(patch_now, 0, patches - 1), 1, keepdims=False
        )
        token_rows = jnp.where(
            section_index == 0, jnp.concatenate([picked, text], axis=1), received
        )
        normed = normalize(token_rows, shift_vec, scale_vec)
        projected = jnp.dot(
            normed.reshape(-1, model_width), weight_qkv, preferred_element_type=jnp.float32
        )
        projected = projected.reshape(requests, row_count, 3, column_count).astype(jnp.bfloat16)
        queries = projected[:, :, 0]
        key_value = projected[:, :, 1:]
        gathered_video, gathered_text = (
            lax.all_gather(key_value[:, :per_dev], "seq", axis=1, tiled=True),
            lax.all_gather(key_value[:, per_dev:], "seq", axis=1, tiled=True),
        )
        current = patch_ids == patch_now
        fresh_video = jnp.where(
            current[None, :, None, None, None], gathered_video[:, None], fresh_video
        )
        fresh_text = jnp.where(patch_now == 0, gathered_text, fresh_text)
        own_video = jnp.where(
            current[None, :, None, None, None], key_value[:, None, :per_dev], own_video
        )
        own_text = jnp.where(patch_now == 0, key_value[:, per_dev:], own_text)
        fresh_all = jnp.concatenate(
            [fresh_video.reshape(requests, patches * capacity, 2, column_count), fresh_text], axis=1
        )
        fresh_mask = all_valid & (all_patch[None, :] <= patch_now)
        query_heads = queries.reshape(requests, row_count, head_count, HEAD)
        scores, value_heads = scores_of(query_heads, fresh_all, head_count)
        fresh_top = masked_max(scores, fresh_mask)
        fresh_sum, fresh_acc = weighed(scores, fresh_mask, fresh_top, value_heads)
        stale_mask = video_valid & (video_patch[None, :] > patch_now)
        scores, value_heads = scores_of(query_heads, stale_whole, head_count)
        stale_top = masked_max(scores, stale_mask)
        stale_sum, stale_acc = weighed(scores, stale_mask, stale_top, value_heads)
        top_score = jnp.maximum(fresh_top, stale_top)
        fresh_weight = jnp.exp(fresh_top - top_score)
        stale_weight = jnp.exp(stale_top - top_score)
        numer = fresh_acc * fresh_weight[..., None] + stale_acc * stale_weight[..., None]
        denom = fresh_sum * fresh_weight + stale_sum * stale_weight
        attended = (numer / denom[..., None]).astype(jnp.bfloat16)
        attended = attended.transpose(0, 2, 1, 3).reshape(requests * row_count, column_count)
        partial_out = jnp.dot(attended, weight_out, preferred_element_type=jnp.float32).reshape(
            requests, row_count, model_width
        )
        summed = lax.psum(partial_out, "mp")
        result = (token_rows.astype(jnp.float32) + gate_vec * summed).astype(jnp.bfloat16)
        out_video = jnp.where(current[None, :, None, None], result[:, None, :per_dev], out_video)
        out_text = jnp.where(patch_now == 0, result[:, per_dev:], out_text)
        if turn_index < patches:
            received = passed_along(result, "section", 1)
    return (out_video[None], out_text[None], own_video[None], own_text[None])


def solution(mesh):
    placed = (
        P(None, None, "seq", None),
        P(None, "seq", None),
        P(),
        P(),
        P(),
        P("section", None, "mp"),
        P("section", None, None, "mp"),
        P("section", "mp", None),
        P("section", None, None, "seq", None, "mp"),
    )
    return jax.shard_map(
        body,
        mesh=mesh,
        in_specs=placed,
        out_specs=(
            P("section", None, None, "seq", None),
            P("section", None, "seq", None),
            P("section", None, None, "seq", None, "mp"),
            P("section", None, "seq", None, "mp"),
        ),
        check_vma=False,
    )
```

profile of v0, /device:TPU:1, one launch (start us, length us, event | category | flops | bytes accessed | tf_op | source)
XLA Modules:
  0.0 716.3 jit_solution(2597853420989053191)
XLA Ops:
  8.0 18.7 %copy.75 = bf16[1,3072,3,768]{1,3,2,0:T(8,128)(2,1)} copy(bf16[1,3072,3,768]{3,1,2,0:T(8,128)(2,1)} %param.15) | data formatting | bytes 28311552 | tf_op args[6]
  35.4 9.3 %fusion.26 = bf16[2,16,3,768]{3,1,2,0:T(8,128)(2,1)S(1)} fusion(bf16[1,3072,3,768]{1,3,2,0:T(8,128)(2,1)} %copy.75, f32[3072]{0:T(1024)S(1)} %get-tuple-element.76, f32[3072]{0:T(1024)S(1)} %get-tuple-element.77, f32[2,16]{1,0:T(2,128)S(1)} %add_rsqrt_fusion.4, f32[2,16]{1,0:T(2,128)S(1)} %broadcast_multiply_fusion.4, ...), kind=kOutput, calls=%fused_computation.57 | convolution fusion | flops 454139904 | bytes 14524673 | tf_op jit(solution)/shard_map/dot_general | solution.py:103
  44.9 24.0 %all_gather.38 = bf16[2,128,2,768]{3,1,2,0:T(8,128)(2,1)S(1)} all-gather(bf16[2,8,2,768]{3,1,2,0:T(8,128)(2,1)S(1)} %get-tuple-element.73), channel_id=1, replica_groups=mesh['section'=2,'seq'=16,'mp'=4] {'seq'}, dimensions={1}, use_global_device_ids=true | all-gather | bytes 835584 | tf_op jit(solution)/shard_map/all_gather | solution.py:111
  70.1 17.7 %all_gather.37 = bf16[2,128,2,768]{3,1,2,0:T(8,128)(2,1)S(1)} all-gather(bf16[2,8,2,768]{3,1,2,0:T(8,128)(2,1)S(1)} %get-tuple-element.74), channel_id=1, replica_groups=mesh['section'=2,'seq'=16,'mp'=4] {'seq'}, dimensions={1}, use_global_device_ids=true | all-gather | bytes 835584 | tf_op jit(solution)/shard_map/all_gather | solution.py:110
  102.9 9.3 %fusion.259 = (bf16[2,512,1,768]{3,2,1,0:T(2,128)(2,1)}, bf16[2,512,1,768]{3,2,1,0:T(2,128)(2,1)}) fusion(bf16[2,512,2,768]{3,2,1,0:T(2,128)(2,1)} %bitcast.353), kind=kLoop, calls=%fused_computation.383 | loop fusion | bytes 6291456 | tf_op jit(solution)/shard_map/slice | solution.py:36
  112.2 6.8 copy.115
  119.0 8.1 %copy.114 = bf16[2,512,1,768]{1,3,0,2:T(8,128)(2,1)} copy(bf16[2,512,1,768]{3,2,1,0:T(2,128)(2,1)} %get-tuple-element.51) | data formatting | bytes 3145728
  135.2 45.4 %all-reduce.7.cloned.1.call-done = f32[2,16,3072]{2,1,0:T(8,128)} async-done(((f32[2,16,3072]{2,1,0:T(8,128)}), f32[2,16,3072]{2,1,0:T(8,128)}) %all-reduce.7.cloned.1.call-update) | async-done | bytes 393232 | tf_op jit(solution)/shard_map/psum | solution.py:144
  190.5 9.3 %fusion.29 = bf16[2,16,3,768]{3,1,2,0:T(8,128)(2,1)S(1)} fusion(bf16[1,3072,3,768]{1,3,2,0:T(8,128)(2,1)} %copy.75, bf16[2,16,3072]{2,1,0:T(8,128)(2,1)S(1)} %get-tuple-element.37, f32[2,16]{1,0:T(2,128)S(1)} %add_rsqrt_fusion.3, f32[2,16]{1,0:T(2,128)S(1)} %broadcast_multiply_fusion.3, f32[3072]{0:T(1024)S(1)} %get-tuple-element.76, ...), kind=kOutput, calls=%fused_computation.58 | convolution fusion | flops 453648384 | bytes 14524672 | tf_op jit(solution)/shard_map/dot_general | solution.py:103
  201.3 19.7 %all_gather.41 = bf16[2,128,2,768]{3,1,2,0:T(8,128)(2,1)S(1)} all-gather(bf16[2,8,2,768]{3,1,2,0:T(8,128)(2,1)S(1)} %get-tuple-element.71), channel_id=1, replica_groups=mesh['section'=2,'seq'=16,'mp'=4] {'seq'}, dimensions={1}, use_global_device_ids=true | all-gather | bytes 835584 | tf_op jit(solution)/shard_map/all_gather | solution.py:111
  222.3 19.1 %all_gather.40 = bf16[2,128,2,768]{3,1,2,0:T(8,128)(2,1)S(1)} all-gather(bf16[2,8,2,768]{3,1,2,0:T(8,128)(2,1)} %get-tuple-element.72), channel_id=1, replica_groups=mesh['section'=2,'seq'=16,'mp'=4] {'seq'}, dimensions={1}, use_global_device_ids=true | all-gather | bytes 835584 | tf_op jit(solution)/shard_map/all_gather | solution.py:110
  264.9 47.4 %all-reduce.9.cloned.1.call-done = f32[2,16,3072]{2,1,0:T(8,128)} async-done(((f32[2,16,3072]{2,1,0:T(8,128)}), f32[2,16,3072]{2,1,0:T(8,128)}) %all-reduce.9.cloned.1.call-update) | async-done | bytes 393232 | tf_op jit(solution)/shard_map/psum | solution.py:144
  322.2 9.3 %fusion.32 = bf16[2,16,3,768]{3,1,2,0:T(8,128)(2,1)S(1)} fusion(bf16[1,3072,3,768]{1,3,2,0:T(8,128)(2,1)} %copy.75, bf16[2,16,3072]{2,1,0:T(8,128)(2,1)S(1)} %get-tuple-element.32, f32[2,16]{1,0:T(2,128)S(1)} %add_rsqrt_fusion.2, f32[2,16]{1,0:T(2,128)S(1)} %broadcast_multiply_fusion.2, f32[3072]{0:T(1024)S(1)} %get-tuple-element.76, ...), kind=kOutput, calls=%fused_computation.59 | convolution fusion | flops 453648384 | bytes 14524672 | tf_op jit(solution)/shard_map/dot_general | solution.py:103
  333.6 19.7 %all_gather.43 = bf16[2,128,2,768]{3,1,2,0:T(8,128)(2,1)S(1)} all-gather(bf16[2,8,2,768]{3,1,2,0:T(8,128)(2,1)S(1)} %get-tuple-element.69), channel_id=1, replica_groups=mesh['section'=2,'seq'=16,'mp'=4] {'seq'}, dimensions={1}, use_global_device_ids=true | all-gather | bytes 835584 | tf_op jit(solution)/shard_map/all_gather | solution.py:111
  354.6 19.2 %all_gather.42 = bf16[2,128,2,768]{3,1,2,0:T(8,128)(2,1)S(1)} all-gather(bf16[2,8,2,768]{3,1,2,0:T(8,128)(2,1)} %get-tuple-element.70), channel_id=1, replica_groups=mesh['section'=2,'seq'=16,'mp'=4] {'seq'}, dimensions={1}, use_global_device_ids=true | all-gather | bytes 835584 | tf_op jit(solution)/shard_map/all_gather | solution.py:110
  397.2 47.5 %all-reduce.11.cloned.1.call-done = f32[2,16,3072]{2,1,0:T(8,128)} async-done(((f32[2,16,3072]{2,1,0:T(8,128)}), f32[2,16,3072]{2,1,0:T(8,128)}) %all-reduce.11.cloned.1.call-update) | async-done | bytes 393232 | tf_op jit(solution)/shard_map/psum | solution.py:144
  454.6 9.3 %fusion.35 = bf16[2,16,3,768]{3,1,2,0:T(8,128)(2,1)S(1)} fusion(bf16[1,3072,3,768]{1,3,2,0:T(8,128)(2,1)} %copy.75, bf16[2,16,3072]{2,1,0:T(8,128)(2,1)S(1)} %get-tuple-element.27, f32[2,16]{1,0:T(2,128)S(1)} %add_rsqrt_fusion.1, f32[2,16]{1,0:T(2,128)S(1)} %broadcast_multiply_fusion.1, f32[3072]{0:T(1024)S(1)} %get-tuple-element.76, ...), kind=kOutput, calls=%fused_computation.60 | convolution fusion | flops 453648384 | bytes 14524672 | tf_op jit(solution)/shard_map/dot_general | solution.py:103
  465.4 19.7 %all_gather.45 = bf16[2,128,2,768]{3,1,2,0:T(8,128)(2,1)S(1)} all-gather(bf16[2,8,2,768]{3,1,2,0:T(8,128)(2,1)S(1)} %get-tuple-element.67), channel_id=1, replica_groups=mesh['section'=2,'seq'=16,'mp'=4] {'seq'}, dimensions={1}, use_global_device_ids=true | all-gather | bytes 835584 | tf_op jit(solution)/shard_map/all_gather | solution.py:111
  486.4 19.2 %all_gather.44 = bf16[2,128,2,768]{3,1,2,0:T(8,128)(2,1)S(1)} all-gather(bf16[2,8,2,768]{3,1,2,0:T(8,128)(2,1)} %get-tuple-element.68), channel_id=1, replica_groups=mesh['section'=2,'seq'=16,'mp'=4] {'seq'}, dimensions={1}, use_global_device_ids=true | all-gather | bytes 835584 | tf_op jit(solution)/shard_map/all_gather | solution.py:110
  529.1 47.4 %all-reduce.13.cloned.1.call-done = f32[2,16,3072]{2,1,0:T(8,128)} async-done(((f32[2,16,3072]{2,1,0:T(8,128)}), f32[2,16,3072]{2,1,0:T(8,128)}) %all-reduce.13.cloned.1.call-update) | async-done | bytes 393232 | tf_op jit(solution)/shard_map/psum | solution.py:144
  586.4 9.3 %fusion.38 = bf16[2,16,3,768]{3,1,2,0:T(8,128)(2,1)S(1)} fusion(bf16[1,3072,3,768]{1,3,2,0:T(8,128)(2,1)} %copy.75, bf16[2,16,3072]{2,1,0:T(8,128)(2,1)S(1)} %get-tuple-element.22, f32[2,16]{1,0:T(2,128)S(1)} %add_rsqrt_fusion, f32[2,16]{1,0:T(2,128)S(1)} %broadcast_multiply_fusion, f32[3072]{0:T(1024)S(1)} %get-tuple-element.76, ...), kind=kOutput, calls=%fused_computation.61 | convolution fusion | flops 453648384 | bytes 14524672 | tf_op jit(solution)/shard_map/dot_general | solution.py:103
  597.4 19.7 %all_gather.47 = bf16[2,128,2,768]{3,1,2,0:T(8,128)(2,1)S(1)} all-gather(bf16[2,8,2,768]{3,1,2,0:T(8,128)(2,1)S(1)} %get-tuple-element.65), channel_id=1, replica_groups=mesh['section'=2,'seq'=16,'mp'=4] {'seq'}, dimensions={1}, use_global_device_ids=true | all-gather | bytes 835584 | tf_op jit(solution)/shard_map/all_gather | solution.py:111
  618.3 19.2 %all_gather.46 = bf16[2,128,2,768]{3,1,2,0:T(8,128)(2,1)S(1)} all-gather(bf16[2,8,2,768]{3,1,2,0:T(8,128)(2,1)} %get-tuple-element.66), channel_id=1, replica_groups=mesh['section'=2,'seq'=16,'mp'=4] {'seq'}, dimensions={1}, use_global_device_ids=true | all-gather | bytes 835584 | tf_op jit(solution)/shard_map/all_gather | solution.py:110
  663.0 43.2 %all-reduce.15.cloned.1.call-done = f32[2,16,3072]{2,1,0:T(8,128)} async-done(((f32[2,16,3072]{2,1,0:T(8,128)}), f32[2,16,3072]{2,1,0:T(8,128)}) %all-reduce.15.cloned.1.call-update) | async-done | bytes 393232 | tf_op jit(solution)/shard_map/psum | solution.py:144
  (295 shorter events, 182.5 us)
Async XLA Ops:
  7.2 95.7 %all-gather.4.cloned.1.call-start = ((), (), s32[]{:S(2)}) async-start(), calls=%async_computation.5 | async-start | bytes 3342336 | tf_op jit(solution)/shard_map/all_gather | solution.py:83
  7.9 172.7 %all-reduce.7.cloned.1.call-start = ((), (), s32[]{:S(2)}) async-start(), calls=%async_computation | async-start | bytes 786432 | tf_op jit(solution)/shard_map/psum | solution.py:144
  8.0 26.3 %copy-start.34 = (bf16[2,4,8,3072]{3,2,1,0:T(8,128)(2,1)S(1)}, bf16[2,4,8,3072]{3,2,1,0:T(8,128)(2,1)}, u32[]{:S(2)}) copy-start(bf16[2,4,8,3072]{3,2,1,0:T(8,128)(2,1)} %param.9) | copy-start | bytes 1179652
  44.7 43.5 %copy-start.22 = (bf16[2,16,3,768]{3,1,2,0:T(8,128)(2,1)}, bf16[2,16,3,768]{3,1,2,0:T(8,128)(2,1)S(1)}, u32[]{:S(2)}) copy-start(bf16[2,16,3,768]{3,1,2,0:T(8,128)(2,1)S(1)} %fusion.26) | copy-start | bytes 442372
  44.9 56.1 %copy-start.18 = (bf16[2,16,12,64]{3,2,1,0:T(8,128)(2,1)}, bf16[2,16,12,64]{3,2,1,0:T(8,128)(2,1)S(1)}, u32[]{:S(2)}) copy-start(bf16[2,16,12,64]{3,2,1,0:T(8,128)(2,1)S(1)} %reshape_squeeze.63) | copy-start | bytes 147460
  131.0 59.1 %copy-start.40 = (bf16[2,8,3072]{2,1,0:T(8,128)(2,1)S(1)}, bf16[2,8,3072]{2,1,0:T(8,128)(2,1)}, u32[]{:S(2)}) copy-start(bf16[2,8,3072]{2,1,0:T(8,128)(2,1)} %get-tuple-element.57) | copy-start | bytes 294916
  135.1 177.3 %all-reduce.9.cloned.1.call-start = ((), (), s32[]{:S(2)}) async-start(), calls=%async_computation.1 | async-start | bytes 786432 | tf_op jit(solution)/shard_map/psum | solution.py:144
  135.2 55.0 %copy-start.46 = (pred[4]{0:T(512)(128)(4,1)}, pred[4]{0:T(512)(128)(4,1)S(1)}, u32[]{:S(2)}) copy-start(pred[4]{0:T(512)(128)(4,1)S(1)} %iota_compare_fusion.3) | copy-start | bytes 16
  181.7 8.4 %collective-permute-start = (bf16[2,16,3072]{2,1,0:T(8,128)(2,1)S(1)}, bf16[2,16,3072]{2,1,0:T(8,128)(2,1)S(1)}, u32[]{:S(2)}, u32[]{:S(2)}) collective-permute-start(bf16[2,16,3072]{2,1,0:T(8,128)(2,1)S(1)} %fusion.136), channel_id=1, source_target_pairs={{0,64},{1,65},{2,66},{3,67},{4,68},{5,69},{6,70},{7,71},{8,72},{9,... | collective-permute-start | bytes 589832 | tf_op jit(solution)/shard_map/ppermute | solution.py:15
  260.8 61.1 %copy-start.39 = (bf16[2,8,3072]{2,1,0:T(8,128)(2,1)S(1)}, bf16[2,8,3072]{2,1,0:T(8,128)(2,1)}, u32[]{:S(2)}) copy-start(bf16[2,8,3072]{2,1,0:T(8,128)(2,1)} %get-tuple-element.54) | copy-start | bytes 294916
  264.8 179.9 %all-reduce.11.cloned.1.call-start = ((), (), s32[]{:S(2)}) async-start(), calls=%async_computation.2 | async-start | bytes 786432 | tf_op jit(solution)/shard_map/psum | solution.py:144
  264.9 57.1 %copy-start.48 = (pred[4]{0:T(512)(128)(4,1)}, pred[4]{0:T(512)(128)(4,1)S(1)}, u32[]{:S(2)}) copy-start(pred[4]{0:T(512)(128)(4,1)S(1)} %iota_compare_fusion.2) | copy-start | bytes 16
  313.4 8.4 %collective-permute-start.1 = (bf16[2,16,3072]{2,1,0:T(8,128)(2,1)S(1)}, bf16[2,16,3072]{2,1,0:T(8,128)(2,1)S(1)}, u32[]{:S(2)}, u32[]{:S(2)}) collective-permute-start(bf16[2,16,3072]{2,1,0:T(8,128)(2,1)S(1)} %fusion.137), channel_id=1, source_target_pairs={{0,64},{1,65},{2,66},{3,67},{4,68},{5,69},{6,70},{7,71},{8,72},{9,... | collective-permute-start | bytes 589832 | tf_op jit(solution)/shard_map/ppermute | solution.py:15
  393.1 61.2 %copy-start.38 = (bf16[2,8,3072]{2,1,0:T(8,128)(2,1)S(1)}, bf16[2,8,3072]{2,1,0:T(8,128)(2,1)}, u32[]{:S(2)}) copy-start(bf16[2,8,3072]{2,1,0:T(8,128)(2,1)} %get-tuple-element.55) | copy-start | bytes 294916
  397.1 179.4 %all-reduce.13.cloned.1.call-start = ((), (), s32[]{:S(2)}) async-start(), calls=%async_computation.3 | async-start | bytes 786432 | tf_op jit(solution)/shard_map/psum | solution.py:144
  445.8 8.4 %collective-permute-start.2 = (bf16[2,16,3072]{2,1,0:T(8,128)(2,1)S(1)}, bf16[2,16,3072]{2,1,0:T(8,128)(2,1)S(1)}, u32[]{:S(2)}, u32[]{:S(2)}) collective-permute-start(bf16[2,16,3072]{2,1,0:T(8,128)(2,1)S(1)} %fusion.138), channel_id=1, source_target_pairs={{0,64},{1,65},{2,66},{3,67},{4,68},{5,69},{6,70},{7,71},{8,72},{9,... | collective-permute-start | bytes 589832 | tf_op jit(solution)/shard_map/ppermute | solution.py:15
  524.9 61.1 %copy-start.37 = (bf16[2,8,3072]{2,1,0:T(8,128)(2,1)S(1)}, bf16[2,8,3072]{2,1,0:T(8,128)(2,1)}, u32[]{:S(2)}) copy-start(bf16[2,8,3072]{2,1,0:T(8,128)(2,1)} %get-tuple-element.53) | copy-start | bytes 294916
  529.0 177.2 %all-reduce.15.cloned.1.call-start = ((), (), s32[]{:S(2)}) async-start(), calls=%async_computation.4 | async-start | bytes 786432 | tf_op jit(solution)/shard_map/psum | solution.py:144
  577.6 8.4 %collective-permute-start.3 = (bf16[2,16,3072]{2,1,0:T(8,128)(2,1)S(1)}, bf16[2,16,3072]{2,1,0:T(8,128)(2,1)S(1)}, u32[]{:S(2)}, u32[]{:S(2)}) collective-permute-start(bf16[2,16,3072]{2,1,0:T(8,128)(2,1)S(1)} %fusion.139), channel_id=1, source_target_pairs={{0,64},{1,65},{2,66},{3,67},{4,68},{5,69},{6,70},{7,71},{8,72},{9,... | collective-permute-start | bytes 589832 | tf_op jit(solution)/shard_map/ppermute | solution.py:15
  654.4 52.9 %copy-start.27 = (bf16[2,16,3072]{2,1,0:T(8,128)(2,1)S(1)}, bf16[2,16,3072]{2,1,0:T(8,128)(2,1)}, u32[]{:S(2)}) copy-start(bf16[2,16,3072]{2,1,0:T(8,128)(2,1)} %copy-done.26) | copy-start | bytes 589828
  654.4 52.9 %copy-start.29 = (bf16[2,16,3072]{2,1,0:T(8,128)(2,1)S(1)}, bf16[2,16,3072]{2,1,0:T(8,128)(2,1)}, u32[]{:S(2)}) copy-start(bf16[2,16,3072]{2,1,0:T(8,128)(2,1)} %copy-done.28) | copy-start | bytes 589828
  654.4 52.9 %copy-start.31 = (bf16[2,16,3072]{2,1,0:T(8,128)(2,1)S(1)}, bf16[2,16,3072]{2,1,0:T(8,128)(2,1)}, u32[]{:S(2)}) copy-start(bf16[2,16,3072]{2,1,0:T(8,128)(2,1)} %copy-done.30) | copy-start | bytes 589828
  654.4 52.9 %copy-start.33 = (bf16[2,16,3072]{2,1,0:T(8,128)(2,1)S(1)}, bf16[2,16,3072]{2,1,0:T(8,128)(2,1)}, u32[]{:S(2)}) copy-start(bf16[2,16,3072]{2,1,0:T(8,128)(2,1)} %copy-done.32) | copy-start | bytes 589828
  654.4 54.5 %copy-start.1 = (bf16[1,512,2304]{2,1,0:T(8,128)(2,1)S(1)}, bf16[1,512,2304]{2,1,0:T(8,128)(2,1)}, u32[]{:S(2)}) copy-start(bf16[1,512,2304]{2,1,0:T(8,128)(2,1)} %param.14) | copy-start | bytes 7077892
  (42 other events, 165.8 us)
Sparse Core Ops, SparseCore 0:
  10.2 52.0 all-gather.3
  135.2 45.3 all-reduce.6
  264.9 47.3 all-reduce.8
  397.3 47.4 all-reduce.10
  529.1 47.3 all-reduce.12
  658.8 47.4 all-reduce.14
where the time goes:
time: 723 us; the launch traced here: 716 us
  waiting for transfers between devices  246 us (34%)
  blocking collectives  203 us (28%)
  local copies, waits for them, and re-layouts  116 us (16%)
  matrix products  86.7 us (12%)
  other arithmetic  30.2 us (4%)
  starting transfers between devices  17.5 us (2%)
  between operations  16.3 us (2%)
    psum x5, waiting for transfers between devices, body(): summed = lax.psum(partial_out, 'mp')  231 us
    all_gather x5, blocking collectives, body(): lax.all_gather(key_value[:, per_dev:], 'seq', axis=1, tiled=True)  103 us
    all_gather x5, blocking collectives, body(): lax.all_gather(key_value[:, :per_dev], 'seq', axis=1, tiled=True)  94.4 us
    broadcast_in_dim x15, local copies, waits for them, and re-layouts, body(): jnp.where(current[None, :, None, None, None], gathered_video[:, None], fr...  47 us
    dot_general x5, matrix products, body(): jnp.dot(normed.reshape(-1, model_width), weight_qkv, preferred_element_ty...  46.6 us
    unnamed x117, local copies, waits for them, and re-layouts  41 us
    dot_general x5, matrix products, body(): jnp.dot(attended, weight_out, preferred_element_type=jnp.float32)  20.3 us
    ppermute x4, starting transfers between devices, passed_along(): lax.ppermute(value, axis, [(source, source + steps) for source in range(l...  17.3 us
  transfers between devices with their start and end apart: 10, of which 9 were waited for; matrix products, arithmetic and copies ran while one was open for 7% of the time, Pallas kernels for 0%

commit v1 on v0

--- a/solution.py
+++ b/solution.py
@@ -3,10 +3,40 @@
 import jax.numpy as jnp
 from jax import lax
 from jax.sharding import PartitionSpec as P
+from jax.lax import axis_index, axis_size, ppermute
 
 HEAD = 64
 EPS = 1e-05
 NEG = -1e30
+
+
+def view_the_rounds(array_in):
+    chip_axis = "seq"
+    block_last, mixed_arr, main = (axis_size(chip_axis), axis_index(chip_axis), array_in.shape[1])
+    blocks_here = []
+    for s, dd in enumerate(array_in.shape):
+        blocks_here.append(dd * block_last if s == 1 else dd)
+    res = lax.dynamic_update_slice_in_dim(
+        jnp.zeros(blocks_here, array_in.dtype), array_in, mixed_arr * main, axis=1
+    )
+    a_next = then = array_in
+    for rr in range(1, block_last // 2 + 1):
+        fields = []
+        for s in range(block_last):
+            fields.append((s, (s + 1) % block_last))
+        a_next = ppermute(a_next, chip_axis, fields)
+        res = lax.dynamic_update_slice_in_dim(
+            res, a_next, (mixed_arr - rr) % block_last * main, axis=1
+        )
+        if 2 * rr < block_last:
+            copies = []
+            for s in range(block_last):
+                copies.append((s, (s - 1) % block_last))
+            then = ppermute(then, chip_axis, copies)
+            res = lax.dynamic_update_slice_in_dim(
+                res, then, (mixed_arr + rr) % block_last * main, axis=1
+            )
+    return res
 
 
 def passed_along(value, axis, steps):
@@ -107,7 +137,7 @@
         queries = projected[:, :, 0]
         key_value = projected[:, :, 1:]
         gathered_video, gathered_text = (
-            lax.all_gather(key_value[:, :per_dev], "seq", axis=1, tiled=True),
+            view_the_rounds(key_value[:, :per_dev]),
             lax.all_gather(key_value[:, per_dev:], "seq", axis=1, tiled=True),
         )
         current = patch_ids == patch_now

time: 723 us -> 889 us (1.23)
  starting transfers between devices: 17.5 us -> 190 us
  blocking collectives: 203 us -> 99 us
  local copies, waits for them, and re-layouts: 116 us -> 163 us
  waiting for transfers between devices: 246 us -> 289 us
    ppermute x0 -> x75, starting transfers between devices: none -> 172 us  [the longest x35 160 us: view_the_rounds(): then = ppermute(then, chip_axis, copies)]
    all_gather x5 -> x0, blocking collectives: 94.4 us -> none  [body(): lax.all_gather(key_value[:, :per_dev], 'seq', axis=1, tiled=True)]
    dynamic_update_slice x0 -> x80, local copies, waits for them, and re-layouts: none -> 50.7 us  [the longest x45 29.8 us: view_the_rounds(): lax.dynamic_update_slice_in_dim(res, a_next, (mixed_arr - rr) % block_las...]
    ppermute x0 -> x75, waiting for transfers between devices: none -> 42.4 us  [the longest x40 42.3 us: view_the_rounds(): a_next = ppermute(a_next, chip_axis, fields)]
    all_gather x5, blocking collectives: 103 us -> 92.6 us  [body(): lax.all_gather(key_value[:, per_dev:], 'seq', axis=1, tiled=True)]
    unnamed x117 -> x147, local copies, waits for them, and re-layouts: 41 us -> 43.7 us
    broadcast_in_dim x15 -> x20, local copies, waits for them, and re-layouts: 47 us -> 44.9 us  [body(): jnp.where(current[None, :, None, None, None], gathered_video[:, None], fr...]
  transfers between devices with their start and end apart: 10 -> 85, of which waited for: 9 -> 36; matrix products, arithmetic and copies ran while one was open for 7% -> 13% of each run, Pallas kernels for 0% -> 0%
where the time goes in v1:
time: 889 us; the launch traced here: 878 us
  waiting for transfers between devices  289 us (33%)
  starting transfers between devices  190 us (21%)
  local copies, waits for them, and re-layouts  163 us (18%)
  blocking collectives  99 us (11%)
  matrix products  86.2 us (10%)
  other arithmetic  34.9 us (4%)
  between operations  16.7 us (2%)
    psum x5, waiting for transfers between devices, body(): summed = lax.psum(partial_out, 'mp')  231 us
    ppermute x35, starting transfers between devices, view_the_rounds(): then = ppermute(then, chip_axis, copies)  160 us
    all_gather x5, blocking collectives, body(): lax.all_gather(key_value[:, per_dev:], 'seq', axis=1, tiled=True)  92.6 us
    dot_general x5, matrix products, body(): jnp.dot(normed.reshape(-1, model_width), weight_qkv, preferred_element_ty...  46.6 us
    broadcast_in_dim x20, local copies, waits for them, and re-layouts, body(): jnp.where(current[None, :, None, None, None], gathered_video[:, None], fr...  44.9 us
    unnamed x147, local copies, waits for them, and re-layouts  43.7 us
    ppermute x40, waiting for transfers between devices, view_the_rounds(): a_next = ppermute(a_next, chip_axis, fields)  42.3 us
    dynamic_update_slice x45, local copies, waits for them, and re-layouts, view_the_rounds(): lax.dynamic_update_slice_in_dim(res, a_next, (mixed_arr - rr) % block_las...  29.8 us
  transfers between devices with their start and end apart: 85, of which 36 were waited for; matrix products, arithmetic and copies ran while one was open for 13% of the time, Pallas kernels for 0%

profile of v1, /device:TPU:1, one launch (start us, length us, event | category | flops | bytes accessed | tf_op | source)
XLA Modules:
  0.0 877.9 jit_solution(17006821328478828570)
XLA Ops:
  8.0 18.7 %copy.75 = bf16[1,3072,3,768]{1,3,2,0:T(8,128)(2,1)} copy(bf16[1,3072,3,768]{3,1,2,0:T(8,128)(2,1)} %param.15) | data formatting | bytes 28311552 | tf_op args[6]
  27.9 6.4 all-gather.1
  35.5 9.3 %fusion.26 = bf16[2,16,3,768]{3,1,2,0:T(8,128)(2,1)S(1)} fusion(bf16[1,3072,3,768]{1,3,2,0:T(8,128)(2,1)} %copy.75, f32[3072]{0:T(1024)S(1)} %get-tuple-element.81, f32[3072]{0:T(1024)S(1)} %get-tuple-element.82, f32[2,16]{1,0:T(2,128)S(1)} %add_rsqrt_fusion.4, f32[2,16]{1,0:T(2,128)S(1)} %broadcast_multiply_fusion.4, ...), kind=kOutput, calls=%fused_computation.57 | convolution fusion | flops 454139904 | bytes 14524673 | tf_op jit(solution)/shard_map/dot_general | solution.py:133
  51.5 19.9 %all_gather.22 = bf16[2,128,2,768]{3,1,2,0:T(8,128)(2,1)S(1)} all-gather(bf16[2,8,2,768]{3,1,2,0:T(8,128)(2,1)S(1)} %get-tuple-element.77), channel_id=1, replica_groups=mesh['section'=2,'seq'=16,'mp'=4] {'seq'}, dimensions={1}, use_global_device_ids=true | all-gather | bytes 835584 | tf_op jit(solution)/shard_map/all_gather | solution.py:141
  112.8 6.2 collective-permute-done.14
  133.2 9.3 %fusion.259 = (bf16[2,512,1,768]{3,2,1,0:T(2,128)(2,1)}, bf16[2,512,1,768]{3,2,1,0:T(2,128)(2,1)}) fusion(bf16[2,512,2,768]{3,2,1,0:T(2,128)(2,1)} %bitcast.353), kind=kLoop, calls=%fused_computation.463 | loop fusion | bytes 6291456 | tf_op jit(solution)/shard_map/slice | solution.py:66
  142.5 6.8 copy.115
  149.3 8.1 copy.114
  165.5 45.3 %all-reduce.7.cloned.1.call-done = f32[2,16,3072]{2,1,0:T(8,128)} async-done(((f32[2,16,3072]{2,1,0:T(8,128)}), f32[2,16,3072]{2,1,0:T(8,128)}) %all-reduce.7.cloned.1.call-update) | async-done | bytes 393232 | tf_op jit(solution)/shard_map/psum | solution.py:174
  220.6 9.3 %fusion.29 = bf16[2,16,3,768]{3,1,2,0:T(8,128)(2,1)S(1)} fusion(bf16[1,3072,3,768]{1,3,2,0:T(8,128)(2,1)} %copy.75, bf16[2,16,3072]{2,1,0:T(8,128)(2,1)S(1)} %get-tuple-element.37, f32[2,16]{1,0:T(2,128)S(1)} %add_rsqrt_fusion.3, f32[2,16]{1,0:T(2,128)S(1)} %broadcast_multiply_fusion.3, f32[3072]{0:T(1024)S(1)} %get-tuple-element.81, ...), kind=kOutput, calls=%fused_computation.58 | convolution fusion | flops 453648384 | bytes 14524672 | tf_op jit(solution)/shard_map/dot_general | solution.py:133
  236.4 18.0 %all_gather.24 = bf16[2,128,2,768]{3,1,2,0:T(8,128)(2,1)S(1)} all-gather(bf16[2,8,2,768]{3,1,2,0:T(8,128)(2,1)} %get-tuple-element.74), channel_id=1, replica_groups=mesh['section'=2,'seq'=16,'mp'=4] {'seq'}, dimensions={1}, use_global_device_ids=true | all-gather | bytes 835584 | tf_op jit(solution)/shard_map/all_gather | solution.py:141
  309.6 5.7 broadcast_in_dim.487
  327.1 47.7 %all-reduce.9.cloned.1.call-done = f32[2,16,3072]{2,1,0:T(8,128)} async-done(((f32[2,16,3072]{2,1,0:T(8,128)}), f32[2,16,3072]{2,1,0:T(8,128)}) %all-reduce.9.cloned.1.call-update) | async-done | bytes 393232 | tf_op jit(solution)/shard_map/psum | solution.py:174
  384.7 9.3 %fusion.32 = bf16[2,16,3,768]{3,1,2,0:T(8,128)(2,1)S(1)} fusion(bf16[1,3072,3,768]{1,3,2,0:T(8,128)(2,1)} %copy.75, bf16[2,16,3072]{2,1,0:T(8,128)(2,1)S(1)} %get-tuple-element.32, f32[2,16]{1,0:T(2,128)S(1)} %add_rsqrt_fusion.2, f32[2,16]{1,0:T(2,128)S(1)} %broadcast_multiply_fusion.2, f32[3072]{0:T(1024)S(1)} %get-tuple-element.81, ...), kind=kOutput, calls=%fused_computation.59 | convolution fusion | flops 453648384 | bytes 14524672 | tf_op jit(solution)/shard_map/dot_general | solution.py:133
  400.7 18.1 %all_gather.25 = bf16[2,128,2,768]{3,1,2,0:T(8,128)(2,1)S(1)} all-gather(bf16[2,8,2,768]{3,1,2,0:T(8,128)(2,1)S(1)} %get-tuple-element.71), channel_id=1, replica_groups=mesh['section'=2,'seq'=16,'mp'=4] {'seq'}, dimensions={1}, use_global_device_ids=true | all-gather | bytes 835584 | tf_op jit(solution)/shard_map/all_gather | solution.py:141
  474.7 5.7 broadcast_in_dim.494
  492.1 47.6 %all-reduce.11.cloned.1.call-done = f32[2,16,3072]{2,1,0:T(8,128)} async-done(((f32[2,16,3072]{2,1,0:T(8,128)}), f32[2,16,3072]{2,1,0:T(8,128)}) %all-reduce.11.cloned.1.call-update) | async-done | bytes 393232 | tf_op jit(solution)/shard_map/psum | solution.py:174
  549.6 9.3 %fusion.35 = bf16[2,16,3,768]{3,1,2,0:T(8,128)(2,1)S(1)} fusion(bf16[1,3072,3,768]{1,3,2,0:T(8,128)(2,1)} %copy.75, bf16[2,16,3072]{2,1,0:T(8,128)(2,1)S(1)} %get-tuple-element.27, f32[2,16]{1,0:T(2,128)S(1)} %add_rsqrt_fusion.1, f32[2,16]{1,0:T(2,128)S(1)} %broadcast_multiply_fusion.1, f32[3072]{0:T(1024)S(1)} %get-tuple-element.81, ...), kind=kOutput, calls=%fused_computation.60 | convolution fusion | flops 453648384 | bytes 14524672 | tf_op jit(solution)/shard_map/dot_general | solution.py:133
  565.5 18.0 %all_gather.26 = bf16[2,128,2,768]{3,1,2,0:T(8,128)(2,1)S(1)} all-gather(bf16[2,8,2,768]{3,1,2,0:T(8,128)(2,1)} %get-tuple-element.68), channel_id=1, replica_groups=mesh['section'=2,'seq'=16,'mp'=4] {'seq'}, dimensions={1}, use_global_device_ids=true | all-gather | bytes 835584 | tf_op jit(solution)/shard_map/all_gather | solution.py:141
  655.9 47.8 %all-reduce.13.cloned.1.call-done = f32[2,16,3072]{2,1,0:T(8,128)} async-done(((f32[2,16,3072]{2,1,0:T(8,128)}), f32[2,16,3072]{2,1,0:T(8,128)}) %all-reduce.13.cloned.1.call-update) | async-done | bytes 393232 | tf_op jit(solution)/shard_map/psum | solution.py:174
  713.5 9.3 %fusion.38 = bf16[2,16,3,768]{3,1,2,0:T(8,128)(2,1)S(1)} fusion(bf16[1,3072,3,768]{1,3,2,0:T(8,128)(2,1)} %copy.75, bf16[2,16,3072]{2,1,0:T(8,128)(2,1)S(1)} %get-tuple-element.22, f32[2,16]{1,0:T(2,128)S(1)} %add_rsqrt_fusion, f32[2,16]{1,0:T(2,128)S(1)} %broadcast_multiply_fusion, f32[3072]{0:T(1024)S(1)} %get-tuple-element.81, ...), kind=kOutput, calls=%fused_computation.61 | convolution fusion | flops 453648384 | bytes 14524672 | tf_op jit(solution)/shard_map/dot_general | solution.py:133
  730.4 18.5 %all_gather.27 = bf16[2,128,2,768]{3,1,2,0:T(8,128)(2,1)S(1)} all-gather(bf16[2,8,2,768]{3,1,2,0:T(8,128)(2,1)S(1)} %get-tuple-element.66), channel_id=1, replica_groups=mesh['section'=2,'seq'=16,'mp'=4] {'seq'}, dimensions={1}, use_global_device_ids=true | all-gather | bytes 835584 | tf_op jit(solution)/shard_map/all_gather | solution.py:141
  803.9 5.7 broadcast_in_dim.508
  825.5 42.6 %all-reduce.15.cloned.1.call-done = f32[2,16,3072]{2,1,0:T(8,128)} async-done(((f32[2,16,3072]{2,1,0:T(8,128)}), f32[2,16,3072]{2,1,0:T(8,128)}) %all-reduce.15.cloned.1.call-update) | async-done | bytes 393232 | tf_op jit(solution)/shard_map/psum | solution.py:174
  (550 shorter events, 418.3 us)
Async XLA Ops:
  7.2 126.0 %all-gather.4.cloned.1.call-start = ((), (), s32[]{:S(2)}) async-start(), calls=%async_computation.5 | async-start | bytes 3342336 | tf_op jit(solution)/shard_map/all_gather | solution.py:113
  7.9 202.8 %all-reduce.7.cloned.1.call-start = ((), (), s32[]{:S(2)}) async-start(), calls=%async_computation | async-start | bytes 786432 | tf_op jit(solution)/shard_map/psum | solution.py:174
  44.9 29.0 %collective-permute-start = (bf16[2,8,2,768]{3,1,2,0:T(8,128)(2,1)S(1)}, bf16[2,8,2,768]{3,1,2,0:T(8,128)(2,1)S(1)}, u32[]{:S(2)}, u32[]{:S(2)}) collective-permute-start(bf16[2,8,2,768]{3,1,2,0:T(8,128)(2,1)S(1)} %get-tuple-element.79), channel_id=1, source_target_pairs={{0,4},{4,8},{8,12},{12,16},{16,20},{20,24},{24,28},{28,32},{32,36}... | collective-permute-start | bytes 147464 | tf_op jit(solution)/shard_map/ppermute | solution.py:27
  46.4 28.4 %collective-permute-start.1 = (bf16[2,8,2,768]{3,1,2,0:T(8,128)(2,1)S(1)}, bf16[2,8,2,768]{3,1,2,0:T(8,128)(2,1)S(1)}, u32[]{:S(2)}, u32[]{:S(2)}) collective-permute-start(bf16[2,8,2,768]{3,1,2,0:T(8,128)(2,1)S(1)} %get-tuple-element.79), channel_id=1, source_target_pairs={{0,60},{4,0},{8,4},{12,8},{16,12},{20,16},{24,20},{28,24},{32,28},... | collective-permute-start | bytes 147464 | tf_op jit(solution)/shard_map/ppermute | solution.py:35
  165.4 209.4 %all-reduce.9.cloned.1.call-start = ((), (), s32[]{:S(2)}) async-start(), calls=%async_computation.1 | async-start | bytes 786432 | tf_op jit(solution)/shard_map/psum | solution.py:174
  211.8 8.4 collective-permute-start.15
  230.7 28.0 %collective-permute-start.16 = (bf16[2,8,2,768]{3,1,2,0:T(8,128)(2,1)}, bf16[2,8,2,768]{3,1,2,0:T(8,128)(2,1)}, u32[]{:S(2)}, u32[]{:S(2)}) collective-permute-start(bf16[2,8,2,768]{3,1,2,0:T(8,128)(2,1)} %get-tuple-element.76), channel_id=1, source_target_pairs={{0,4},{4,8},{8,12},{12,16},{16,20},{20,24},{24,28},{28,32},{32,36}... | collective-permute-start | bytes 147464 | tf_op jit(solution)/shard_map/ppermute | solution.py:27
  231.9 29.2 %collective-permute-start.17 = (bf16[2,8,2,768]{3,1,2,0:T(8,128)(2,1)}, bf16[2,8,2,768]{3,1,2,0:T(8,128)(2,1)}, u32[]{:S(2)}, u32[]{:S(2)}) collective-permute-start(bf16[2,8,2,768]{3,1,2,0:T(8,128)(2,1)} %get-tuple-element.76), channel_id=1, source_target_pairs={{0,60},{4,0},{8,4},{12,8},{16,12},{20,16},{24,20},{28,24},{32,28},... | collective-permute-start | bytes 147464 | tf_op jit(solution)/shard_map/ppermute | solution.py:35
  258.7 7.9 collective-permute-start.18
  327.0 212.8 %all-reduce.11.cloned.1.call-start = ((), (), s32[]{:S(2)}) async-start(), calls=%async_computation.2 | async-start | bytes 786432 | tf_op jit(solution)/shard_map/psum | solution.py:174
  375.9 8.4 collective-permute-start.31
  395.6 28.0 %collective-permute-start.32 = (bf16[2,8,2,768]{3,1,2,0:T(8,128)(2,1)S(1)}, bf16[2,8,2,768]{3,1,2,0:T(8,128)(2,1)}, u32[]{:S(2)}, u32[]{:S(2)}) collective-permute-start(bf16[2,8,2,768]{3,1,2,0:T(8,128)(2,1)S(1)} %get-tuple-element.73), channel_id=1, source_target_pairs={{0,4},{4,8},{8,12},{12,16},{16,20},{20,24},{24,28},{28,32},{32,36}... | collective-permute-start | bytes 147464 | tf_op jit(solution)/shard_map/ppermute | solution.py:27
  396.8 29.4 %collective-permute-start.33 = (bf16[2,8,2,768]{3,1,2,0:T(8,128)(2,1)S(1)}, bf16[2,8,2,768]{3,1,2,0:T(8,128)(2,1)}, u32[]{:S(2)}, u32[]{:S(2)}) collective-permute-start(bf16[2,8,2,768]{3,1,2,0:T(8,128)(2,1)S(1)} %get-tuple-element.73), channel_id=1, source_target_pairs={{0,60},{4,0},{8,4},{12,8},{16,12},{20,16},{24,20},{28,24},{32,28},... | collective-permute-start | bytes 147464 | tf_op jit(solution)/shard_map/ppermute | solution.py:35
  423.6 7.7 collective-permute-start.34
  492.1 211.6 %all-reduce.13.cloned.1.call-start = ((), (), s32[]{:S(2)}) async-start(), calls=%async_computation.3 | async-start | bytes 786432 | tf_op jit(solution)/shard_map/psum | solution.py:174
  540.8 8.4 collective-permute-start.47
  559.7 28.0 %collective-permute-start.48 = (bf16[2,8,2,768]{3,1,2,0:T(8,128)(2,1)}, bf16[2,8,2,768]{3,1,2,0:T(8,128)(2,1)}, u32[]{:S(2)}, u32[]{:S(2)}) collective-permute-start(bf16[2,8,2,768]{3,1,2,0:T(8,128)(2,1)} %get-tuple-element.70), channel_id=1, source_target_pairs={{0,4},{4,8},{8,12},{12,16},{16,20},{20,24},{24,28},{28,32},{32,36}... | collective-permute-start | bytes 147464 | tf_op jit(solution)/shard_map/ppermute | solution.py:27
  560.9 29.0 %collective-permute-start.49 = (bf16[2,8,2,768]{3,1,2,0:T(8,128)(2,1)}, bf16[2,8,2,768]{3,1,2,0:T(8,128)(2,1)}, u32[]{:S(2)}, u32[]{:S(2)}) collective-permute-start(bf16[2,8,2,768]{3,1,2,0:T(8,128)(2,1)} %get-tuple-element.70), channel_id=1, source_target_pairs={{0,60},{4,0},{8,4},{12,8},{16,12},{20,16},{24,20},{28,24},{32,28},... | collective-permute-start | bytes 147464 | tf_op jit(solution)/shard_map/ppermute | solution.py:35
  587.8 7.7 collective-permute-start.50
  655.8 212.2 %all-reduce.15.cloned.1.call-start = ((), (), s32[]{:S(2)}) async-start(), calls=%async_computation.4 | async-start | bytes 786432 | tf_op jit(solution)/shard_map/psum | solution.py:174
  704.7 8.4 collective-permute-start.63
  725.4 27.6 %collective-permute-start.64 = (bf16[2,8,2,768]{3,1,2,0:T(8,128)(2,1)S(1)}, bf16[2,8,2,768]{3,1,2,0:T(8,128)(2,1)}, u32[]{:S(2)}, u32[]{:S(2)}) collective-permute-start(bf16[2,8,2,768]{3,1,2,0:T(8,128)(2,1)S(1)} %get-tuple-element.67), channel_id=1, source_target_pairs={{0,4},{4,8},{8,12},{12,16},{16,20},{20,24},{24,28},{28,32},{32,36}... | collective-permute-start | bytes 147464 | tf_op jit(solution)/shard_map/ppermute | solution.py:27
  726.6 28.9 %collective-permute-start.65 = (bf16[2,8,2,768]{3,1,2,0:T(8,128)(2,1)S(1)}, bf16[2,8,2,768]{3,1,2,0:T(8,128)(2,1)}, u32[]{:S(2)}, u32[]{:S(2)}) collective-permute-start(bf16[2,8,2,768]{3,1,2,0:T(8,128)(2,1)S(1)} %get-tuple-element.67), channel_id=1, source_target_pairs={{0,60},{4,0},{8,4},{12,8},{16,12},{20,16},{24,20},{28,24},{32,28},... | collective-permute-start | bytes 147464 | tf_op jit(solution)/shard_map/ppermute | solution.py:35
  753.0 7.7 collective-permute-start.66
  (132 other events, 1851.1 us)
Sparse Core Ops, SparseCore 0:
  10.2 51.7 all-gather.3
  165.5 45.1 all-reduce.6
  327.1 47.6 all-reduce.8
  492.2 47.5 all-reduce.10
  655.9 47.6 all-reduce.12
  820.4 47.5 all-reduce.14
